TPU v7x, 32 devices: a whole 2x2x4 slice. The times are simulated.
32 devices in a mesh: row: 4 (over z), col: 2 (over x), rep: 4 (over y, core).
Axes of the slice: x: 2, y: 2, z: 4, core: 2. Of those that a mesh axis runs over, the one named last changes fastest.
Arguments:
- features: bfloat16 [8192, 256], P(('col', 'rep'), 'row'), may hold values from -6 to 6
- weight: bfloat16 [256, 256], replicated, may hold values from -0.375 to 0.375
- cotangent: bfloat16 [8192, 256], P(('row', 'col', 'rep')), may hold values from -6 to 6
- block_values: bfloat16 [4, 8, 128, 128, 128], P('row', ('col', 'rep')), may hold values from -0.0625 to 0.0625
- block_coords: int32 [4, 8, 128, 2], P('row', ('col', 'rep')), may hold values from 0 to 15, as said below
- block_counts: int32 [4, 8], P('row', ('col', 'rep')), may hold values from 1 to 128, as said below
Outputs:
- activations: bfloat16 [8192, 256], P(('row', 'col', 'rep'))
- input_grad: bfloat16 [8192, 256], P(('col', 'rep'), 'row')
- weight_grad: float32 [256, 256], replicated
Inputs may be any that keep to these rules, and one draw needn't show every extreme that they name: `block_coords`: each slot's row block is below 16 and its column block below 8. `block_counts`: some tile uses all 128 slots.
All inputs are finite; a program needn't handle non-finite values.
Results may differ from a plain program's by a relative error of at most 0.014.
Values may be sent and summed in bfloat16 or wider, within the bound.
A program may use at most 128 MiB of HBM per device.

v0:
```python
import math
import jax
import jax.numpy as jnp
from jax import lax
from jax.sharding import PartitionSpec as P


def local(features, weight, cotangent, block_values, block_coords, block_counts):
    blocks = block_values[0, 0]
    coords = block_coords[0, 0]
    live_count = block_counts[0, 0]
    slots = blocks.shape[0]
    gathered = lax.all_gather(features, "row", axis=1, tiled=True)
    feat_width = gathered.shape[1]
    col_blocks = gathered.shape[0] // 128
    row_blocks = cotangent.shape[0] * lax.axis_size(("col", "rep")) // 128
    feat_blocks = gathered.reshape(col_blocks, 128, feat_width)
    is_live = (jnp.arange(slots, dtype=jnp.int32) < live_count).astype(jnp.float32)
    per_turn = math.gcd(slots, 64)
    rounds = slots // per_turn
    pieces = (
        blocks.reshape(rounds, per_turn, 128, 128),
        coords[:, 0].reshape(rounds, per_turn),
        coords[:, 1].reshape(rounds, per_turn),
        is_live.reshape(rounds, per_turn),
    )

    def forward_step(total, piece):
        blocks_g, rows_g, cols_g, live_g = piece
        chosen = feat_blocks[cols_g]
        product = jnp.einsum("bij,bjf->bif", blocks_g, chosen, preferred_element_type=jnp.float32)
        return (total.at[rows_g].add(product * live_g[:, None, None]), None)

    partial_value, _ = lax.scan(
        forward_step, jnp.zeros((row_blocks, 128, feat_width), jnp.float32), pieces
    )
    partial_value = partial_value.reshape(row_blocks * 128, feat_width)
    summed = lax.psum_scatter(partial_value, ("col", "rep"), scatter_dimension=0, tiled=True)
    aggregate = summed.astype(jnp.bfloat16)
    pre_act = jnp.dot(aggregate, weight, preferred_element_type=jnp.float32)
    sigma = jax.nn.sigmoid(pre_act)
    activations = (pre_act * sigma).astype(jnp.bfloat16)
    grad_pre = (cotangent.astype(jnp.float32) * sigma * (1.0 + pre_act * (1.0 - sigma))).astype(
        jnp.bfloat16
    )
    weight_terms = jnp.dot(aggregate.T, grad_pre, preferred_element_type=jnp.float32)
    share = lax.psum_scatter(
        weight_terms.astype(jnp.bfloat16), ("col", "rep"), scatter_dimension=0, tiled=True
    ).astype(jnp.float32)
    share = lax.psum(share, "row")
    weight_grad = lax.all_gather(share, ("col", "rep"), axis=0, tiled=True)
    back_rows = jnp.dot(grad_pre, weight.T, preferred_element_type=jnp.float32).astype(jnp.bfloat16)
    back_all = lax.all_gather(back_rows, ("col", "rep"), axis=0, tiled=True)
    back_blocks = back_all.reshape(row_blocks, 128, back_all.shape[1])

    def backward_step(total, piece):
        blocks_g, rows_g, cols_g, live_g = piece
        chosen = back_blocks[rows_g]
        product = jnp.einsum("bji,bjf->bif", blocks_g, chosen, preferred_element_type=jnp.float32)
        return (total.at[cols_g].add(product * live_g[:, None, None]), None)

    grad_terms, _ = lax.scan(
        backward_step, jnp.zeros((col_blocks, 128, back_all.shape[1]), jnp.float32), pieces
    )
    grad_terms = grad_terms.reshape(col_blocks * 128, back_all.shape[1])
    input_grad = lax.psum_scatter(
        grad_terms.astype(jnp.bfloat16), "row", scatter_dimension=1, tiled=True
    )
    return (activations, input_grad, weight_grad)


def solution(mesh):
    in_specs = (
        P(("col", "rep"), "row"),
        P(),
        P(("row", "col", "rep"), None),
        P("row", ("col", "rep"), None, None, None),
        P("row", ("col", "rep"), None, None),
        P("row", ("col", "rep")),
    )
    out_specs = (P(("row", "col", "rep"), None), P(("col", "rep"), "row"), P())
    return jax.shard_map(local, mesh=mesh, in_specs=in_specs, out_specs=out_specs, check_vma=False)
```

profile of v0, /device:TPU:0, one launch (start us, length us, event | category | flops | bytes accessed | tf_op | source)
XLA Modules:
  0.0 228.0 jit_solution(13461801693741192329)
XLA Ops:
  8.8 17.6 %all_gather.9 = bf16[1024,256]{0,1:T(8,128)(2,1)S(1)} all-gather(bf16[1024,64]{0,1:T(8,128)(2,1)} %param.10), channel_id=1, replica_groups=mesh['row'=4,'col'=2,'rep'=4] {'row'}, dimensions={1}, use_global_device_ids=true | all-gather | bytes 655360 | tf_op jit(solution)/shard_map/all_gather | solution.py:13
  26.8 45.1 %while.20 = (s32[]{:T(128)}, f32[16,128,256]{2,1,0:T(8,128)S(1)}, s32[2,64]{1,0:T(2,128)S(1)}, bf16[2,64,128,128]{3,2,1,0:T(8,128)(2,1)}, s32[2,64]{1,0:T(2,128)...) while((s32[]{:T(128)}, f32[16,128,256]{2,1,0:T(8,128)S(1)}, ...), condition=%wide.region_2.3_spmd, body=%wide.region_0.2_spmd.sunk | while | flops 541066624 | bytes 48241756 | solution.py:34
  26.9 2.8 %gather_fusion = bf16[64,128,256]{2,1,0:T(8,128)(2,1)} fusion(bf16[8,128,256]{2,1,0:T(8,128)(2,1)S(1)} %get-tuple-element.237, s32[1024]{0:T(1024)S(1)} %pad_clamp_fusion.4), kind=kCustom, calls=%fused_computation.clone.1 | custom fusion | bytes 8388864 | tf_op jit(solution)/shard_map/while/body/eval_jaxpr/gather | solution.py:30
  29.7 7.3 %broadcast_multiply_fusion.4 = f32[64,128,256]{2,1,0:T(8,128)} fusion(f32[64]{0:T(128)S(1)} %fusion.36, bf16[64,128,256]{2,1,0:T(8,128)(2,1)} %gather_fusion, bf16[2,64,128,128]{3,2,1,0:T(8,128)(2,1)} %get-tuple-element.235, s32[]{:T(128)} %get-tuple-element.224), kind=kOutput, calls=%fused_computation.4.clone.1 | convolution fusion | flops 538968064 | bytes 14680832 | tf_op jit(solution)/shard_map/while/body/eval_jaxpr/bij,bjf->bif/dot_general | solution.py:31
  37.0 12.4 %scatter_fusion = f32[16,128,256]{2,1,0:T(8,128)S(1)} fusion(f32[16,128,256]{2,1,0:T(8,128)S(1)} %get-tuple-element.225, s32[64]{0:T(128)S(1)} %get-tuple-element.205, f32[64,128,256]{2,1,0:T(8,128)} %broadcast_multiply_fusion.4), kind=kCustom, calls=%fused_computation.2.clone.1 | custom fusion | flops 2097152 | bytes 25166080 | tf_op jit(solution)/shard_map/while/body/eval_jaxpr/scatter-add | solution.py:32
  49.4 2.8 %gather_fusion = bf16[64,128,256]{2,1,0:T(8,128)(2,1)} fusion(bf16[8,128,256]{2,1,0:T(8,128)(2,1)S(1)} %get-tuple-element.237, s32[1024]{0:T(1024)S(1)} %pad_clamp_fusion.4), kind=kCustom, calls=%fused_computation.clone.1 | custom fusion | bytes 8388864 | tf_op jit(solution)/shard_map/while/body/eval_jaxpr/gather | solution.py:30
  52.2 7.3 %broadcast_multiply_fusion.4 = f32[64,128,256]{2,1,0:T(8,128)} fusion(f32[64]{0:T(128)S(1)} %fusion.36, bf16[64,128,256]{2,1,0:T(8,128)(2,1)} %gather_fusion, bf16[2,64,128,128]{3,2,1,0:T(8,128)(2,1)} %get-tuple-element.235, s32[]{:T(128)} %get-tuple-element.224), kind=kOutput, calls=%fused_computation.4.clone.1 | convolution fusion | flops 538968064 | bytes 14680832 | tf_op jit(solution)/shard_map/while/body/eval_jaxpr/bij,bjf->bif/dot_general | solution.py:31
  59.5 12.4 %scatter_fusion = f32[16,128,256]{2,1,0:T(8,128)S(1)} fusion(f32[16,128,256]{2,1,0:T(8,128)S(1)} %get-tuple-element.225, s32[64]{0:T(128)S(1)} %get-tuple-element.205, f32[64,128,256]{2,1,0:T(8,128)} %broadcast_multiply_fusion.4), kind=kCustom, calls=%fused_computation.2.clone.1 | custom fusion | flops 2097152 | bytes 25166080 | tf_op jit(solution)/shard_map/while/body/eval_jaxpr/scatter-add | solution.py:32
  72.0 1.3 copy-done.1
  73.4 43.0 %reduce-scatter.4.cloned.1.call-done = f32[256,256]{1,0:T(8,128)} async-done(((f32[2048,256]{1,0:T(8,128)}), f32[256,256]{1,0:T(8,128)}) %reduce-scatter.4.cloned.1.call-update) | async-done | bytes 262160 | tf_op jit(solution)/shard_map/reduce_scatter | solution.py:38
  116.4 1.9 multiply_convert_fusion
  119.2 6.4 %copy.9 = bf16[1,1,128,128,128]{3,4,2,1,0:T(8,128)(2,1)} copy(bf16[1,1,128,128,128]{4,3,2,1,0:T(8,128)(2,1)} %bitcast.81) | data formatting | bytes 8388608 | tf_op args[3]
  125.6 0.9 convolution_convert_fusion
  126.6 16.1 %all-gather.2.cloned.1.call-done = bf16[2048,256]{1,0:T(8,128)(2,1)} async-done(((bf16[256,256]{1,0:T(8,128)(2,1)}), bf16[2048,256]{1,0:T(8,128)(2,1)}) %all-gather.2.cloned.1.call-update) | async-done | bytes 1048592 | tf_op jit(solution)/shard_map/all_gather | solution.py:53
  142.8 47.4 %while.21 = (s32[]{:T(128)}, f32[8,128,256]{2,1,0:T(8,128)S(1)}, s32[2,64]{1,0:T(2,128)S(1)}, bf16[2,64,128,128]{2,3,1,0:T(8,128)(2,1)}, s32[2,64]{1,0:T(2,128)S...) while((s32[]{:T(128)}, f32[8,128,256]{2,1,0:T(8,128)S(1)}, s32[2,64]{1,0:T(2,128)S(1)}, ...), condition=%wide.region_6.7_spmd, body=%wide.region_4.6_spmd.sunk | while | flops 541066624 | bytes 48241756 | solution.py:62
  142.8 4.0 %gather_fusion.1 = bf16[64,128,256]{2,1,0:T(8,128)(2,1)} fusion(bf16[16,128,256]{2,1,0:T(8,128)(2,1)} %get-tuple-element.261, s32[1024]{0:T(1024)S(1)} %pad_clamp_fusion.5), kind=kCustom, calls=%fused_computation.1.clone.1 | custom fusion | bytes 8388864 | tf_op jit(solution)/shard_map/while/body/eval_jaxpr/gather | solution.py:58
  146.8 7.3 %broadcast_multiply_fusion.5 = f32[64,128,256]{2,1,0:T(8,128)} fusion(f32[64]{0:T(128)S(1)} %fusion.40, bf16[64,128,256]{2,1,0:T(8,128)(2,1)} %gather_fusion.1, bf16[2,64,128,128]{2,3,1,0:T(8,128)(2,1)} %get-tuple-element.259, s32[]{:T(128)} %get-tuple-element.248), kind=kOutput, calls=%fused_computation.19.clone.1 | convolution fusion | flops 538968064 | bytes 14680832 | tf_op jit(solution)/shard_map/while/body/eval_jaxpr/bji,bjf->bif/dot_general | solution.py:59
  154.1 12.4 %scatter_fusion.1 = f32[8,128,256]{2,1,0:T(8,128)S(1)} fusion(f32[8,128,256]{2,1,0:T(8,128)S(1)} %get-tuple-element.249, s32[64]{0:T(128)S(1)} %get-tuple-element.214, f32[64,128,256]{2,1,0:T(8,128)} %broadcast_multiply_fusion.5), kind=kCustom, calls=%fused_computation.3.clone.1 | custom fusion | flops 2097152 | bytes 25166080 | tf_op jit(solution)/shard_map/while/body/eval_jaxpr/scatter-add | solution.py:60
  166.5 4.0 %gather_fusion.1 = bf16[64,128,256]{2,1,0:T(8,128)(2,1)} fusion(bf16[16,128,256]{2,1,0:T(8,128)(2,1)} %get-tuple-element.261, s32[1024]{0:T(1024)S(1)} %pad_clamp_fusion.5), kind=kCustom, calls=%fused_computation.1.clone.1 | custom fusion | bytes 8388864 | tf_op jit(solution)/shard_map/while/body/eval_jaxpr/gather | solution.py:58
  170.6 7.3 %broadcast_multiply_fusion.5 = f32[64,128,256]{2,1,0:T(8,128)} fusion(f32[64]{0:T(128)S(1)} %fusion.40, bf16[64,128,256]{2,1,0:T(8,128)(2,1)} %gather_fusion.1, bf16[2,64,128,128]{2,3,1,0:T(8,128)(2,1)} %get-tuple-element.259, s32[]{:T(128)} %get-tuple-element.248), kind=kOutput, calls=%fused_computation.19.clone.1 | convolution fusion | flops 538968064 | bytes 14680832 | tf_op jit(solution)/shard_map/while/body/eval_jaxpr/bji,bjf->bif/dot_general | solution.py:59
  177.8 12.4 %scatter_fusion.1 = f32[8,128,256]{2,1,0:T(8,128)S(1)} fusion(f32[8,128,256]{2,1,0:T(8,128)S(1)} %get-tuple-element.249, s32[64]{0:T(128)S(1)} %get-tuple-element.214, f32[64,128,256]{2,1,0:T(8,128)} %broadcast_multiply_fusion.5), kind=kCustom, calls=%fused_computation.3.clone.1 | custom fusion | flops 2097152 | bytes 25166080 | tf_op jit(solution)/shard_map/while/body/eval_jaxpr/scatter-add | solution.py:60
  190.3 1.0 copy.14
  191.4 20.2 %psum.7 = f32[32,256]{1,0:T(8,128)S(1)} all-reduce(bf16[32,256]{1,0:T(8,128)(2,1)} %reduce-scatter.8.cloned.1.call-done), channel_id=1, replica_groups=mesh['row'=4,'col'=2,'rep'=4] {'row'}, use_global_device_ids=true, to_apply=%region_9.10 | all-reduce | flops 8192 | bytes 49152 | tf_op jit(solution)/shard_map/psum | solution.py:50
  211.6 9.2 %all_gather.11 = f32[256,256]{1,0:T(8,128)S(1)} all-gather(f32[32,256]{1,0:T(8,128)S(1)} %psum.7), channel_id=1, replica_groups=mesh['row'=4,'col'=2,'rep'=4] {'col','rep'}, dimensions={0}, use_global_device_ids=true | all-gather | bytes 294912 | tf_op jit(solution)/shard_map/all_gather | solution.py:51
  (39 shorter events, 3.4 us)
Async XLA Ops:
  7.2 109.2 %copy-start = (bf16[256,256]{1,0:T(8,128)(2,1)S(1)}, bf16[256,256]{1,0:T(8,128)(2,1)}, u32[]{:S(2)}) copy-start(bf16[256,256]{1,0:T(8,128)(2,1)} %param.11) | copy-start | bytes 393220
  7.2 109.2 %reduce-scatter.4.cloned.1.call-start = ((), (), s32[]{:S(2)}) async-start(), calls=%async_computation.3 | async-start | bytes 2359296 | tf_op jit(solution)/shard_map/reduce_scatter | solution.py:38
  26.8 89.6 %copy-start.3 = (bf16[256,256]{1,0:T(8,128)(2,1)S(1)}, bf16[256,256]{1,0:T(8,128)(2,1)}, u32[]{:S(2)}) copy-start(bf16[256,256]{1,0:T(8,128)(2,1)} %param.12) | copy-start | bytes 393220
  71.9 1.4 copy-start.1
  73.3 69.4 %all-gather.2.cloned.1.call-start = ((), (), s32[]{:S(2)}) async-start(), calls=%async_computation.4 | async-start | bytes 1179648 | tf_op jit(solution)/shard_map/all_gather | solution.py:53
  119.2 6.5 %copy-start.2 = (f32[256,256]{1,0:T(8,128)S(1)}, f32[256,256]{1,0:T(8,128)}, u32[]{:S(2)}) copy-start(f32[256,256]{1,0:T(8,128)} %reduce-scatter.4.cloned.1.call-done) | copy-start | bytes 786436
  119.2 72.1 %reduce-scatter.8.cloned.1.call-start = ((), (), s32[]{:S(2)}) async-start(), calls=%async_computation.6 | async-start | bytes 147456 | tf_op jit(solution)/shard_map/reduce_scatter | solution.py:47
  126.5 94.3 %reduce-scatter.6.cloned.1.call-start = ((), (), s32[]{:S(2)}) async-start(), calls=%async_computation.5 | async-start | bytes 655360 | tf_op jit(solution)/shard_map/reduce_scatter | solution.py:66
Sparse Core Ops, SparseCore 0:
  73.4 42.9 reduce-scatter.3
  119.3 23.3 all-gather.1
  146.3 33.5 reduce-scatter.7
  191.4 22.2 reduce-scatter.5
where the time goes:
time: 229 us; the launch traced here: 228 us
  waiting for transfers between devices  59.2 us (26%)
  other arithmetic  49.7 us (22%)
  blocking collectives  47 us (21%)
  matrix products  32.8 us (14%)
  local copies, waits for them, and re-layouts  24.5 us (11%)
  between operations  14.5 us (6%)
    reduce_scatter x1, waiting for transfers between devices, local(): lax.psum_scatter(partial_value, ('col', 'rep'), scatter_dimension=0, tile...  43 us
    scatter-add x2, other arithmetic, forward_step(): return (total.at[rows_g].add(product * live_g[:, None, None]), None)  24.8 us
    scatter-add x2, other arithmetic, backward_step(): return (total.at[cols_g].add(product * live_g[:, None, None]), None)  24.8 us
    psum x1, blocking collectives, local(): share = lax.psum(share, 'row')  20.2 us
    all_gather x1, blocking collectives, local(): gathered = lax.all_gather(features, 'row', axis=1, tiled=True)  17.6 us
    all_gather x1, waiting for transfers between devices, local(): back_all = lax.all_gather(back_rows, ('col', 'rep'), axis=0, tiled=True)  16.1 us
    dot_general x2, matrix products, forward_step(): jnp.einsum('bij,bjf->bif', blocks_g, chosen, preferred_element_type=jnp.f...  14.6 us
    dot_general x2, matrix products, backward_step(): jnp.einsum('bji,bjf->bif', blocks_g, chosen, preferred_element_type=jnp.f...  14.6 us
  transfers between devices with their start and end apart: 4, of which 2 were waited for; matrix products, arithmetic and copies ran while one was open for 24% of the time, Pallas kernels for 0%

commit v1 on v0

--- a/solution.py
+++ b/solution.py
@@ -47,7 +47,9 @@
     share = lax.psum_scatter(
         weight_terms.astype(jnp.bfloat16), ("col", "rep"), scatter_dimension=0, tiled=True
     ).astype(jnp.float32)
-    share = lax.psum(share, "row")
+    share = share
+    for hop in (1, 2):
+        share = share + lax.ppermute(share, "row", [(dev, dev ^ hop) for dev in range(4)])
     weight_grad = lax.all_gather(share, ("col", "rep"), axis=0, tiled=True)
     back_rows = jnp.dot(grad_pre, weight.T, preferred_element_type=jnp.float32).astype(jnp.bfloat16)
     back_all = lax.all_gather(back_rows, ("col", "rep"), axis=0, tiled=True)

time: 229 us -> 222 us (0.969)
  blocking collectives: 47 us -> 26.8 us
  waiting for transfers between devices: 59.2 us -> 66.9 us
  starting transfers between devices: 0.16 us -> 4.06 us
    psum x1 -> x0, blocking collectives: 20.2 us -> none  [local(): share = lax.psum(share, 'row')]
    ppermute x0 -> x2, waiting for transfers between devices: none -> 6.57 us  [local(): lax.ppermute(share, 'row', [(dev, dev ^ hop) for dev in range(4)])]
    ppermute x0 -> x2, starting transfers between devices: none -> 3.9 us  [local(): lax.ppermute(share, 'row', [(dev, dev ^ hop) for dev in range(4)])]
  transfers between devices with their start and end apart: 4 -> 6, of which waited for: 2 -> 5; matrix products, arithmetic and copies ran while one was open for 24% -> 26% of each run, Pallas kernels for 0% -> 0%
where the time goes in v1:
time: 222 us; the launch traced here: 221 us
  waiting for transfers between devices  66.9 us (30%)
  other arithmetic  51.2 us (23%)
  matrix products  32.8 us (15%)
  blocking collectives  26.8 us (12%)
  local copies, waits for them, and re-layouts  24.4 us (11%)
  between operations  14.5 us (7%)
  starting transfers between devices  4.06 us (2%)
    reduce_scatter x1, waiting for transfers between devices, local(): lax.psum_scatter(partial_value, ('col', 'rep'), scatter_dimension=0, tile...  43 us
    scatter-add x2, other arithmetic, forward_step(): return (total.at[rows_g].add(product * live_g[:, None, None]), None)  24.8 us
    scatter-add x2, other arithmetic, backward_step(): return (total.at[cols_g].add(product * live_g[:, None, None]), None)  24.8 us
    all_gather x1, blocking collectives, local(): gathered = lax.all_gather(features, 'row', axis=1, tiled=True)  17.6 us
    all_gather x1, waiting for transfers between devices, local(): back_all = lax.all_gather(back_rows, ('col', 'rep'), axis=0, tiled=True)  16.1 us
    dot_general x2, matrix products, backward_step(): jnp.einsum('bji,bjf->bif', blocks_g, chosen, preferred_element_type=jnp.f...  14.6 us
    dot_general x2, matrix products, forward_step(): jnp.einsum('bij,bjf->bif', blocks_g, chosen, preferred_element_type=jnp.f...  14.6 us
    all_gather x1, blocking collectives, local(): weight_grad = lax.all_gather(share, ('col', 'rep'), axis=0, tiled=True)  9.21 us
  transfers between devices with their start and end apart: 6, of which 5 were waited for; matrix products, arithmetic and copies ran while one was open for 26% of the time, Pallas kernels for 0%

profile of v1, /device:TPU:0, one launch (start us, length us, event | category | flops | bytes accessed | tf_op | source)
XLA Modules:
  0.0 220.8 jit_solution(10059310440463415122)
XLA Ops:
  8.8 17.6 %all_gather.9 = bf16[1024,256]{0,1:T(8,128)(2,1)S(1)} all-gather(bf16[1024,64]{0,1:T(8,128)(2,1)} %param.10), channel_id=1, replica_groups=mesh['row'=4,'col'=2,'rep'=4] {'row'}, dimensions={1}, use_global_device_ids=true | all-gather | bytes 655360 | tf_op jit(solution)/shard_map/all_gather | solution.py:13
  26.8 45.0 %while.20 = (s32[]{:T(128)}, f32[16,128,256]{2,1,0:T(8,128)S(1)}, s32[2,64]{1,0:T(2,128)S(1)}, bf16[2,64,128,128]{3,2,1,0:T(8,128)(2,1)}, s32[2,64]{1,0:T(2,128)...) while((s32[]{:T(128)}, f32[16,128,256]{2,1,0:T(8,128)S(1)}, ...), condition=%wide.region_2.3_spmd, body=%wide.region_0.2_spmd.sunk | while | flops 541066624 | bytes 48241756 | solution.py:34
  26.9 2.8 %gather_fusion = bf16[64,128,256]{2,1,0:T(8,128)(2,1)} fusion(bf16[8,128,256]{2,1,0:T(8,128)(2,1)S(1)} %get-tuple-element.237, s32[1024]{0:T(1024)S(1)} %pad_clamp_fusion.4), kind=kCustom, calls=%fused_computation.clone.1 | custom fusion | bytes 8388864 | tf_op jit(solution)/shard_map/while/body/eval_jaxpr/gather | solution.py:30
  29.6 7.3 %broadcast_multiply_fusion.4 = f32[64,128,256]{2,1,0:T(8,128)} fusion(f32[64]{0:T(128)S(1)} %fusion.36, bf16[64,128,256]{2,1,0:T(8,128)(2,1)} %gather_fusion, bf16[2,64,128,128]{3,2,1,0:T(8,128)(2,1)} %get-tuple-element.235, s32[]{:T(128)} %get-tuple-element.224), kind=kOutput, calls=%fused_computation.4.clone.1 | convolution fusion | flops 538968064 | bytes 14680832 | tf_op jit(solution)/shard_map/while/body/eval_jaxpr/bij,bjf->bif/dot_general | solution.py:31
  36.9 12.4 %scatter_fusion = f32[16,128,256]{2,1,0:T(8,128)S(1)} fusion(f32[16,128,256]{2,1,0:T(8,128)S(1)} %get-tuple-element.225, s32[64]{0:T(128)S(1)} %get-tuple-element.205, f32[64,128,256]{2,1,0:T(8,128)} %broadcast_multiply_fusion.4), kind=kCustom, calls=%fused_computation.2.clone.1 | custom fusion | flops 2097152 | bytes 25166080 | tf_op jit(solution)/shard_map/while/body/eval_jaxpr/scatter-add | solution.py:32
  49.4 2.8 %gather_fusion = bf16[64,128,256]{2,1,0:T(8,128)(2,1)} fusion(bf16[8,128,256]{2,1,0:T(8,128)(2,1)S(1)} %get-tuple-element.237, s32[1024]{0:T(1024)S(1)} %pad_clamp_fusion.4), kind=kCustom, calls=%fused_computation.clone.1 | custom fusion | bytes 8388864 | tf_op jit(solution)/shard_map/while/body/eval_jaxpr/gather | solution.py:30
  52.2 7.3 %broadcast_multiply_fusion.4 = f32[64,128,256]{2,1,0:T(8,128)} fusion(f32[64]{0:T(128)S(1)} %fusion.36, bf16[64,128,256]{2,1,0:T(8,128)(2,1)} %gather_fusion, bf16[2,64,128,128]{3,2,1,0:T(8,128)(2,1)} %get-tuple-element.235, s32[]{:T(128)} %get-tuple-element.224), kind=kOutput, calls=%fused_computation.4.clone.1 | convolution fusion | flops 538968064 | bytes 14680832 | tf_op jit(solution)/shard_map/while/body/eval_jaxpr/bij,bjf->bif/dot_general | solution.py:31
  59.5 12.4 %scatter_fusion = f32[16,128,256]{2,1,0:T(8,128)S(1)} fusion(f32[16,128,256]{2,1,0:T(8,128)S(1)} %get-tuple-element.225, s32[64]{0:T(128)S(1)} %get-tuple-element.205, f32[64,128,256]{2,1,0:T(8,128)} %broadcast_multiply_fusion.4), kind=kCustom, calls=%fused_computation.2.clone.1 | custom fusion | flops 2097152 | bytes 25166080 | tf_op jit(solution)/shard_map/while/body/eval_jaxpr/scatter-add | solution.py:32
  73.3 43.0 %reduce-scatter.4.cloned.1.call-done = f32[256,256]{1,0:T(8,128)} async-done(((f32[2048,256]{1,0:T(8,128)}), f32[256,256]{1,0:T(8,128)}) %reduce-scatter.4.cloned.1.call-update) | async-done | bytes 262160 | tf_op jit(solution)/shard_map/reduce_scatter | solution.py:38
  116.3 1.9 multiply_convert_fusion
  119.2 6.4 %copy.9 = bf16[1,1,128,128,128]{3,4,2,1,0:T(8,128)(2,1)} copy(bf16[1,1,128,128,128]{4,3,2,1,0:T(8,128)(2,1)} %bitcast.81) | data formatting | bytes 8388608 | tf_op args[3]
  126.5 16.1 %all-gather.2.cloned.1.call-done = bf16[2048,256]{1,0:T(8,128)(2,1)} async-done(((bf16[256,256]{1,0:T(8,128)(2,1)}), bf16[2048,256]{1,0:T(8,128)(2,1)}) %all-gather.2.cloned.1.call-update) | async-done | bytes 1048592 | tf_op jit(solution)/shard_map/all_gather | solution.py:55
  142.7 47.4 %while.21 = (s32[]{:T(128)}, f32[8,128,256]{2,1,0:T(8,128)S(1)}, s32[2,64]{1,0:T(2,128)S(1)}, bf16[2,64,128,128]{2,3,1,0:T(8,128)(2,1)}, s32[2,64]{1,0:T(2,128)S...) while((s32[]{:T(128)}, f32[8,128,256]{2,1,0:T(8,128)S(1)}, s32[2,64]{1,0:T(2,128)S(1)}, ...), condition=%wide.region_6.7_spmd, body=%wide.region_4.6_spmd.sunk | while | flops 541066624 | bytes 48241756 | solution.py:64
  142.7 4.0 %gather_fusion.1 = bf16[64,128,256]{2,1,0:T(8,128)(2,1)} fusion(bf16[16,128,256]{2,1,0:T(8,128)(2,1)} %get-tuple-element.261, s32[1024]{0:T(1024)S(1)} %pad_clamp_fusion.5), kind=kCustom, calls=%fused_computation.1.clone.1 | custom fusion | bytes 8388864 | tf_op jit(solution)/shard_map/while/body/eval_jaxpr/gather | solution.py:60
  146.7 7.3 %broadcast_multiply_fusion.5 = f32[64,128,256]{2,1,0:T(8,128)} fusion(f32[64]{0:T(128)S(1)} %fusion.40, bf16[64,128,256]{2,1,0:T(8,128)(2,1)} %gather_fusion.1, bf16[2,64,128,128]{2,3,1,0:T(8,128)(2,1)} %get-tuple-element.259, s32[]{:T(128)} %get-tuple-element.248), kind=kOutput, calls=%fused_computation.19.clone.1 | convolution fusion | flops 538968064 | bytes 14680832 | tf_op jit(solution)/shard_map/while/body/eval_jaxpr/bji,bjf->bif/dot_general | solution.py:61
  154.0 12.4 %scatter_fusion.1 = f32[8,128,256]{2,1,0:T(8,128)S(1)} fusion(f32[8,128,256]{2,1,0:T(8,128)S(1)} %get-tuple-element.249, s32[64]{0:T(128)S(1)} %get-tuple-element.214, f32[64,128,256]{2,1,0:T(8,128)} %broadcast_multiply_fusion.5), kind=kCustom, calls=%fused_computation.3.clone.1 | custom fusion | flops 2097152 | bytes 25166080 | tf_op jit(solution)/shard_map/while/body/eval_jaxpr/scatter-add | solution.py:62
  166.4 4.0 %gather_fusion.1 = bf16[64,128,256]{2,1,0:T(8,128)(2,1)} fusion(bf16[16,128,256]{2,1,0:T(8,128)(2,1)} %get-tuple-element.261, s32[1024]{0:T(1024)S(1)} %pad_clamp_fusion.5), kind=kCustom, calls=%fused_computation.1.clone.1 | custom fusion | bytes 8388864 | tf_op jit(solution)/shard_map/while/body/eval_jaxpr/gather | solution.py:60
  170.4 7.3 %broadcast_multiply_fusion.5 = f32[64,128,256]{2,1,0:T(8,128)} fusion(f32[64]{0:T(128)S(1)} %fusion.40, bf16[64,128,256]{2,1,0:T(8,128)(2,1)} %gather_fusion.1, bf16[2,64,128,128]{2,3,1,0:T(8,128)(2,1)} %get-tuple-element.259, s32[]{:T(128)} %get-tuple-element.248), kind=kOutput, calls=%fused_computation.19.clone.1 | convolution fusion | flops 538968064 | bytes 14680832 | tf_op jit(solution)/shard_map/while/body/eval_jaxpr/bji,bjf->bif/dot_general | solution.py:61
  177.7 12.4 %scatter_fusion.1 = f32[8,128,256]{2,1,0:T(8,128)S(1)} fusion(f32[8,128,256]{2,1,0:T(8,128)S(1)} %get-tuple-element.249, s32[64]{0:T(128)S(1)} %get-tuple-element.214, f32[64,128,256]{2,1,0:T(8,128)} %broadcast_multiply_fusion.5), kind=kCustom, calls=%fused_computation.3.clone.1 | custom fusion | flops 2097152 | bytes 25166080 | tf_op jit(solution)/shard_map/while/body/eval_jaxpr/scatter-add | solution.py:62
  191.9 1.5 collective-permute-start
  193.4 2.4 %collective-permute-done = f32[32,256]{1,0:T(8,128)S(1)} collective-permute-done((f32[32,256]{1,0:T(8,128)S(1)}, f32[32,256]{1,0:T(8,128)S(1)}, u32[]{:S(2)}, u32[]{:S(2)}) %collective-permute-start) | collective-permute-done | bytes 32800 | tf_op jit(solution)/shard_map/ppermute | solution.py:52
  196.6 2.4 %collective-permute-start.1 = (f32[32,256]{1,0:T(8,128)S(1)}, f32[32,256]{1,0:T(8,128)S(1)}, u32[]{:S(2)}, u32[]{:S(2)}) collective-permute-start(f32[32,256]{1,0:T(8,128)S(1)} %convert_add_fusion), channel_id=1, source_target_pairs={{0,16},{8,24},{16,0},{24,8},{1,17},{9,25},{17,1},{25,9},{2,18},{10... | collective-permute-start | bytes 98312 | tf_op jit(solution)/shard_map/ppermute | solution.py:52
  199.0 4.1 %collective-permute-done.1 = f32[32,256]{1,0:T(8,128)S(1)} collective-permute-done((f32[32,256]{1,0:T(8,128)S(1)}, f32[32,256]{1,0:T(8,128)S(1)}, u32[]{:S(2)}, u32[]{:S(2)}) %collective-permute-start.1) | collective-permute-done | bytes 32800 | tf_op jit(solution)/shard_map/ppermute | solution.py:52
  203.1 9.2 %all_gather.11 = f32[256,256]{1,0:T(8,128)S(1)} all-gather(f32[32,256]{1,0:T(8,128)S(1)} %add.72), channel_id=1, replica_groups=mesh['row'=4,'col'=2,'rep'=4] {'col','rep'}, dimensions={0}, use_global_device_ids=true | all-gather | bytes 294912 | tf_op jit(solution)/shard_map/all_gather | solution.py:53
  (45 shorter events, 9.2 us)
Async XLA Ops:
  7.2 109.1 %copy-start = (bf16[256,256]{1,0:T(8,128)(2,1)S(1)}, bf16[256,256]{1,0:T(8,128)(2,1)}, u32[]{:S(2)}) copy-start(bf16[256,256]{1,0:T(8,128)(2,1)} %param.11) | copy-start | bytes 393220
  7.2 109.1 %reduce-scatter.4.cloned.1.call-start = ((), (), s32[]{:S(2)}) async-start(), calls=%async_computation.3 | async-start | bytes 2359296 | tf_op jit(solution)/shard_map/reduce_scatter | solution.py:38
  26.8 89.5 %copy-start.3 = (bf16[256,256]{1,0:T(8,128)(2,1)S(1)}, bf16[256,256]{1,0:T(8,128)(2,1)}, u32[]{:S(2)}) copy-start(bf16[256,256]{1,0:T(8,128)(2,1)} %param.12) | copy-start | bytes 393220
  71.9 1.3 copy-start.1
  73.2 69.4 %all-gather.2.cloned.1.call-start = ((), (), s32[]{:S(2)}) async-start(), calls=%async_computation.4 | async-start | bytes 1179648 | tf_op jit(solution)/shard_map/all_gather | solution.py:55
  119.1 6.5 %copy-start.2 = (f32[256,256]{1,0:T(8,128)S(1)}, f32[256,256]{1,0:T(8,128)}, u32[]{:S(2)}) copy-start(f32[256,256]{1,0:T(8,128)} %reduce-scatter.4.cloned.1.call-done) | copy-start | bytes 786436
  119.1 72.1 %reduce-scatter.8.cloned.1.call-start = ((), (), s32[]{:S(2)}) async-start(), calls=%async_computation.6 | async-start | bytes 147456 | tf_op jit(solution)/shard_map/reduce_scatter | solution.py:47
  126.5 87.1 %reduce-scatter.6.cloned.1.call-start = ((), (), s32[]{:S(2)}) async-start(), calls=%async_computation.5 | async-start | bytes 655360 | tf_op jit(solution)/shard_map/reduce_scatter | solution.py:68
  191.9 3.9 %collective-permute-start = (f32[32,256]{1,0:T(8,128)S(1)}, f32[32,256]{1,0:T(8,128)S(1)}, u32[]{:S(2)}, u32[]{:S(2)}) collective-permute-start(f32[32,256]{1,0:T(8,128)S(1)} %convert_element_type.40), channel_id=1, source_target_pairs={{0,8},{8,0},{16,24},{24,16},{1,9},{9,1},{17,25},{25,17},{2,10},{10... | collective-permute-start | bytes 98312 | tf_op jit(solution)/shard_map/ppermute | solution.py:52
  196.6 6.6 %collective-permute-start.1 = (f32[32,256]{1,0:T(8,128)S(1)}, f32[32,256]{1,0:T(8,128)S(1)}, u32[]{:S(2)}, u32[]{:S(2)}) collective-permute-start(f32[32,256]{1,0:T(8,128)S(1)} %convert_add_fusion), channel_id=1, source_target_pairs={{0,16},{8,24},{16,0},{24,8},{1,17},{9,25},{17,1},{25,9},{2,18},{10... | collective-permute-start | bytes 98312 | tf_op jit(solution)/shard_map/ppermute | solution.py:52
Sparse Core Ops, SparseCore 0:
  73.4 42.9 reduce-scatter.3
  119.2 23.3 all-gather.1
  146.2 33.5 reduce-scatter.7
  191.3 22.1 reduce-scatter.5
